TPU v7x, 32 devices: a whole 2x2x4 slice. The times are simulated.
32 devices in a mesh: wide: 8 (over z, x), narrow: 4 (over y, core).
Axes of the slice: x: 2, y: 2, z: 4, core: 2. Of those that a mesh axis runs over, the one named last changes fastest.
Arguments:
- latents: bfloat16 [128, 32, 32, 384], P('wide', 'narrow'), may hold values from -6 to 6
- timesteps: int32 [128], P('wide'), may hold values from 0 to 999
- out_grad: bfloat16 [128, 16, 16, 768], P(('wide', 'narrow')), may hold values from -6 to 6
- ada_weight: bfloat16 [256, 2304], replicated, may hold values from -1 to 1
- ada_bias: bfloat16 [2304], replicated, may hold values from -4 to 4
- conv_attn: bfloat16 [3, 3, 384], replicated, may hold values from -2 to 2
- qkv_weight: bfloat16 [384, 1152], replicated, may hold values from -0.3125 to 0.3125
- proj_weight: bfloat16 [384, 384], replicated, may hold values from -1.25 to 1.25
- fc1_weight: bfloat16 [384, 1536], replicated, may hold values from -0.3125 to 0.3125
- fc1_bias: bfloat16 [1536], replicated, may hold values from -6 to 6
- conv_ffn: bfloat16 [3, 3, 1536], replicated, may hold values from -2 to 2
- fc2_weight: bfloat16 [1536, 384], replicated, may hold values from -0.15625 to 0.15625
- fc2_bias: bfloat16 [384], replicated, may hold values from -4 to 4
- down_weight: bfloat16 [1536, 768], replicated, may hold values from -0.15625 to 0.15625
- down_bias: bfloat16 [768], replicated, may hold values from -4 to 4
Outputs:
- result: bfloat16 [128, 16, 16, 768], P(('wide', 'narrow'))
- grad_latents: float32 [128, 32, 32, 384], P('wide', 'narrow')
- grad_ada_weight: float32 [256, 2304], replicated
- grad_ada_bias: float32 [2304], replicated
- grad_conv_attn: float32 [3, 3, 384], replicated
- grad_qkv_weight: float32 [384, 1152], replicated
- grad_proj_weight: float32 [384, 384], replicated
- grad_fc1_weight: float32 [384, 1536], replicated
- grad_fc1_bias: float32 [1536], replicated
- grad_conv_ffn: float32 [3, 3, 1536], replicated
- grad_fc2_weight: float32 [1536, 384], replicated
- grad_fc2_bias: float32 [384], replicated
- grad_down_weight: float32 [1536, 768], replicated
- grad_down_bias: float32 [768], replicated
All inputs are finite; a program needn't handle non-finite values.
Results may differ from a plain program's by a relative error of at most 0.018.
The roundings to bfloat16 on the way count: a program that leaves them out, or rounds other values in their place, can miss the bound.
Values may be sent and summed in bfloat16 or wider, within the bound.
No kernel may reach another device: no remote copies, remote signals or barrier semaphores. Data moves between devices by JAX's collectives and lax.ppermute only.
A program may use at most 384 MiB of HBM per device.

v0:
```python
import math
import jax
import jax.numpy as jnp
from jax import lax
from jax.sharding import PartitionSpec as P

HEADS = 6
EPSILON = 1e-06
HIGH = lax.Precision.HIGHEST


def with_halo(block, sides, width):
    for axis, dim in sides:
        count = lax.axis_size(axis)
        forward = [(i, i + 1) for i in range(count - 1)]
        backward = [(target, source) for source, target in forward]
        low = lax.ppermute(
            lax.slice_in_dim(block, block.shape[dim] - width, None, axis=dim), axis, forward
        )
        high = lax.ppermute(lax.slice_in_dim(block, 0, width, axis=dim), axis, backward)
        block = jnp.concatenate([low, block, high], axis=dim)
    return block


def timestep_features(steps_in, feature_count):
    half_count = feature_count // 2
    freq_table = jnp.exp(
        -math.log(10000.0) * jnp.arange(half_count, dtype=jnp.float32) / half_count
    )
    angles = steps_in.astype(jnp.float32)[:, None] * freq_table[None, :]
    return jnp.concatenate([jnp.cos(angles), jnp.sin(angles)], axis=1)


def layer_norm(values):
    center = values - jnp.mean(values, axis=-1, keepdims=True)
    spread = jnp.mean(center * center, axis=-1, keepdims=True)
    return center * lax.rsqrt(spread + EPSILON)


def modulate_norm(values, shift_part, scale_part):
    return layer_norm(values) * (1.0 + scale_part) + shift_part


def gelu_tanh(values):
    return jax.nn.gelu(values, approximate=True)


def depth_conv(row_padded, kernel):
    row_count = row_padded.shape[1] - 2
    col_count = row_padded.shape[2]
    padded = jnp.pad(row_padded, ((0, 0), (0, 0), (1, 1), (0, 0)))
    total = jnp.zeros((row_padded.shape[0], row_count, col_count, row_padded.shape[3]), jnp.float32)
    for row_tap in range(3):
        for col_tap in range(3):
            window = padded[
                :, row_tap : row_tap + row_count, col_tap : col_tap + col_count, :
            ].astype(jnp.float32)
            total = total + window * kernel[row_tap, col_tap].astype(jnp.float32)
    return total


def depth_conv_grads(row_padded, grad_padded, kernel):
    row_count = grad_padded.shape[1] - 2
    col_count = grad_padded.shape[2]
    inputs_full = jnp.pad(row_padded, ((0, 0), (0, 0), (1, 1), (0, 0)))
    grads_full = jnp.pad(grad_padded, ((0, 0), (0, 0), (1, 1), (0, 0)))
    centre = grad_padded[:, 1 : 1 + row_count, :, :].astype(jnp.float32)
    input_grad = jnp.zeros(centre.shape, jnp.float32)
    kernel_rows = []
    for row_tap in range(3):
        tap_list = []
        for col_tap in range(3):
            window = inputs_full[
                :, row_tap : row_tap + row_count, col_tap : col_tap + col_count, :
            ].astype(jnp.float32)
            tap_list.append(jnp.sum(window * centre, axis=(0, 1, 2)))
            mirror = grads_full[
                :, 2 - row_tap : 2 - row_tap + row_count, 2 - col_tap : 2 - col_tap + col_count, :
            ].astype(jnp.float32)
            input_grad = input_grad + mirror * kernel[row_tap, col_tap].astype(jnp.float32)
        kernel_rows.append(jnp.stack(tap_list))
    return (jnp.stack(kernel_rows), input_grad)


def to_groups(values, head_count):
    batch_size, row_count, col_count, channels = values.shape
    head_size = channels // head_count
    shaped = values.reshape(batch_size, row_count // 2, 2, col_count // 2, 2, head_count, head_size)
    shaped = shaped.transpose(0, 2, 4, 5, 1, 3, 6)
    return shaped.reshape(batch_size, 4, head_count, row_count // 2 * (col_count // 2), head_size)


def from_groups(values, row_count, col_count):
    batch_size = values.shape[0]
    head_count = values.shape[2]
    head_size = values.shape[4]
    shaped = values.reshape(batch_size, 2, 2, head_count, row_count // 2, col_count // 2, head_size)
    shaped = shaped.transpose(0, 4, 1, 5, 2, 3, 6)
    return shaped.reshape(batch_size, row_count, col_count, head_count * head_size)


def unshuffle(values):
    batch_size, row_count, col_count, channels = values.shape
    shaped = values.reshape(batch_size, row_count // 2, 2, col_count // 2, 2, channels)
    return shaped.transpose(0, 1, 3, 2, 4, 5).reshape(
        batch_size, row_count // 2, col_count // 2, 4 * channels
    )


def shuffle(values):
    batch_size, half_rows, half_cols, wide_channels = values.shape
    channels = wide_channels // 4
    shaped = values.reshape(batch_size, half_rows, half_cols, 2, 2, channels)
    return shaped.transpose(0, 1, 3, 2, 4, 5).reshape(
        batch_size, 2 * half_rows, 2 * half_cols, channels
    )


def attend_scores(q_groups, k_groups):
    factor = q_groups.shape[-1] ** (-0.5)
    return (
        jnp.einsum("bghqe,bghke->bghqk", q_groups, k_groups, preferred_element_type=jnp.float32)
        * factor
    )


def shards(
    latents,
    timesteps,
    out_grad,
    ada_weight,
    ada_bias,
    conv_attn,
    qkv_weight,
    proj_weight,
    fc1_weight,
    fc1_bias,
    conv_ffn,
    fc2_weight,
    fc2_bias,
    down_weight,
    down_bias,
):
    channels = latents.shape[3]
    cond_all = jax.nn.silu(timestep_features(timesteps, ada_weight.shape[0])).astype(jnp.bfloat16)
    mod_all = jnp.dot(cond_all, ada_weight, preferred_element_type=jnp.float32) + ada_bias.astype(
        jnp.float32
    )
    image_count = latents.shape[0]
    row_count = latents.shape[1]
    col_count = latents.shape[2]
    pieces = [
        mod_all[:, None, None, part_index * channels : (part_index + 1) * channels]
        for part_index in range(6)
    ]
    shift_one, scale_one, gate_one, shift_two, scale_two, gate_two = pieces
    values_in = latents.astype(jnp.float32)
    hidden_in = modulate_norm(values_in, shift_one, scale_one).astype(jnp.bfloat16)
    padded_in = with_halo(hidden_in, (("narrow", 1),), 1)
    conv_out = depth_conv(padded_in, conv_attn).astype(jnp.bfloat16)
    qkv_all = jnp.dot(conv_out, qkv_weight, preferred_element_type=jnp.float32)
    query_own = qkv_all[..., :channels].astype(jnp.bfloat16)
    pair_own = qkv_all[..., channels:].astype(jnp.bfloat16)
    pair_all = lax.all_gather(pair_own, "narrow", axis=1, tiled=True)
    key_rows = pair_all.shape[1]
    q_groups = to_groups(query_own, HEADS)
    k_groups = to_groups(pair_all[..., :channels], HEADS)
    v_groups = to_groups(pair_all[..., channels:], HEADS)
    scores = attend_scores(q_groups, k_groups)
    top_score = jnp.max(scores, axis=-1, keepdims=True)
    log_total = top_score + jnp.log(jnp.sum(jnp.exp(scores - top_score), axis=-1, keepdims=True))
    probs_low = jnp.exp(scores - log_total).astype(jnp.bfloat16)
    mixed_groups = jnp.einsum(
        "bghqk,bghke->bghqe", probs_low, v_groups, preferred_element_type=jnp.float32
    )
    mixed = from_groups(mixed_groups, row_count, col_count).astype(jnp.bfloat16)
    attn_out = jnp.dot(mixed, proj_weight, preferred_element_type=jnp.float32)
    after_attn = values_in + gate_one * attn_out
    hidden_two = modulate_norm(after_attn, shift_two, scale_two).astype(jnp.bfloat16)
    ffn_pre = (
        jnp.dot(hidden_two, fc1_weight, preferred_element_type=jnp.float32)
        + fc1_bias.astype(jnp.float32)
    ).astype(jnp.bfloat16)
    padded_ffn = with_halo(ffn_pre, (("narrow", 1),), 1)
    ffn_conv = depth_conv(padded_ffn, conv_ffn)
    activated = gelu_tanh(ffn_conv).astype(jnp.bfloat16)
    ffn_out = jnp.dot(activated, fc2_weight, preferred_element_type=jnp.float32) + fc2_bias.astype(
        jnp.float32
    )
    after_ffn = after_attn + gate_two * ffn_out
    low_res = unshuffle(after_ffn).astype(jnp.bfloat16)
    result_own = (
        jnp.dot(low_res, down_weight, preferred_element_type=jnp.float32)
        + down_bias.astype(jnp.float32)
    ).astype(jnp.bfloat16)
    result = lax.all_to_all(result_own, "narrow", split_axis=0, concat_axis=1, tiled=True)
    grad_low = lax.all_to_all(out_grad, "narrow", split_axis=1, concat_axis=0, tiled=True)
    grad_down_weight = jnp.einsum(
        "bijc,bijo->co", low_res, grad_low, preferred_element_type=jnp.float32
    )
    grad_down_bias = jnp.sum(grad_low.astype(jnp.float32), axis=(0, 1, 2))
    grad_after = shuffle(
        jnp.einsum("bijo,co->bijc", grad_low, down_weight, preferred_element_type=jnp.float32)
    )
    grad_ffn_out = (gate_two * grad_after).astype(jnp.bfloat16)
    grad_gate_two = jnp.sum(ffn_out * grad_after, axis=(1, 2))
    grad_fc2_weight = jnp.einsum(
        "brwf,brwd->fd", activated, grad_ffn_out, preferred_element_type=jnp.float32
    )
    grad_fc2_bias = jnp.sum(grad_ffn_out.astype(jnp.float32), axis=(0, 1, 2))
    grad_act = jnp.einsum(
        "brwd,fd->brwf", grad_ffn_out, fc2_weight, preferred_element_type=jnp.float32
    )
    unused_gelu, gelu_back = jax.vjp(gelu_tanh, ffn_conv)
    grad_conv = gelu_back(grad_act)[0].astype(jnp.bfloat16)
    grad_conv_pad = with_halo(grad_conv, (("narrow", 1),), 1)
    grad_conv_ffn, grad_pre = depth_conv_grads(padded_ffn, grad_conv_pad, conv_ffn)
    grad_pre_low = grad_pre.astype(jnp.bfloat16)
    grad_fc1_weight = jnp.einsum(
        "brwd,brwf->df", hidden_two, grad_pre_low, preferred_element_type=jnp.float32
    )
    grad_fc1_bias = jnp.sum(grad_pre_low.astype(jnp.float32), axis=(0, 1, 2))
    grad_hidden_two = jnp.einsum(
        "brwf,df->brwd", grad_pre_low, fc1_weight, preferred_element_type=jnp.float32
    )
    unused_two, norm_back_two = jax.vjp(modulate_norm, after_attn, shift_two, scale_two)
    grad_from_two, grad_shift_two, grad_scale_two = norm_back_two(grad_hidden_two)
    grad_mid = grad_after + grad_from_two
    grad_attn_out = (gate_one * grad_mid).astype(jnp.bfloat16)
    grad_gate_one = jnp.sum(attn_out * grad_mid, axis=(1, 2))
    grad_proj_weight = jnp.einsum(
        "brwd,brwe->de", mixed, grad_attn_out, preferred_element_type=jnp.float32
    )
    grad_mixed = jnp.einsum(
        "brwe,de->brwd", grad_attn_out, proj_weight, preferred_element_type=jnp.float32
    ).astype(jnp.bfloat16)
    grad_mixed_groups = to_groups(grad_mixed, HEADS)
    scores_again = attend_scores(q_groups, k_groups)
    probs_again = jnp.exp(scores_again - log_total)
    probs_again_low = probs_again.astype(jnp.bfloat16)
    grad_probs = jnp.einsum(
        "bghqe,bghke->bghqk", grad_mixed_groups, v_groups, preferred_element_type=jnp.float32
    )
    grad_value_groups = jnp.einsum(
        "bghqk,bghqe->bghke", probs_again_low, grad_mixed_groups, preferred_element_type=jnp.float32
    )
    inner_sum = jnp.sum(probs_again * grad_probs, axis=-1, keepdims=True)
    grad_scores = (probs_again * (grad_probs - inner_sum)).astype(jnp.bfloat16)
    factor = q_groups.shape[-1] ** (-0.5)
    grad_query_groups = factor * jnp.einsum(
        "bghqk,bghke->bghqe", grad_scores, k_groups, preferred_element_type=jnp.float32
    )
    grad_key_groups = factor * jnp.einsum(
        "bghqk,bghqe->bghke", grad_scores, q_groups, preferred_element_type=jnp.float32
    )
    grad_pair = jnp.concatenate(
        [
            from_groups(grad_key_groups, key_rows, col_count),
            from_groups(grad_value_groups, key_rows, col_count),
        ],
        axis=-1,
    )
    grad_pair_own = lax.psum_scatter(
        grad_pair.astype(jnp.bfloat16), "narrow", scatter_dimension=1, tiled=True
    ).astype(jnp.float32)
    grad_qkv = jnp.concatenate(
        [from_groups(grad_query_groups, row_count, col_count), grad_pair_own], axis=-1
    ).astype(jnp.bfloat16)
    grad_qkv_weight = jnp.einsum(
        "brwd,brwe->de", conv_out, grad_qkv, preferred_element_type=jnp.float32
    )
    grad_conv_out = jnp.einsum(
        "brwe,de->brwd", grad_qkv, qkv_weight, preferred_element_type=jnp.float32
    ).astype(jnp.bfloat16)
    grad_conv_out_pad = with_halo(grad_conv_out, (("narrow", 1),), 1)
    grad_conv_attn, grad_hidden_in = depth_conv_grads(padded_in, grad_conv_out_pad, conv_attn)
    unused_one, norm_back_one = jax.vjp(modulate_norm, values_in, shift_one, scale_one)
    grad_from_one, grad_shift_one, grad_scale_one = norm_back_one(grad_hidden_in)
    grad_tokens = grad_mid + grad_from_one
    grad_modulation = jnp.concatenate(
        [
            grad_shift_one.reshape(image_count, channels),
            grad_scale_one.reshape(image_count, channels),
            grad_gate_one,
            grad_shift_two.reshape(image_count, channels),
            grad_scale_two.reshape(image_count, channels),
            grad_gate_two,
        ],
        axis=1,
    )
    grad_ada_weight = jnp.dot(cond_all.astype(jnp.float32).T, grad_modulation, precision=HIGH)
    grad_ada_bias = jnp.sum(grad_modulation, axis=0)
    totals = lax.psum(
        (
            grad_ada_weight,
            grad_ada_bias,
            grad_conv_attn,
            grad_qkv_weight,
            grad_proj_weight,
            grad_fc1_weight,
            grad_fc1_bias,
            grad_conv_ffn,
            grad_fc2_weight,
            grad_fc2_bias,
            grad_down_weight,
            grad_down_bias,
        ),
        ("wide", "narrow"),
    )
    return (
        result,
        grad_tokens,
        totals[0],
        totals[1],
        totals[2],
        totals[3],
        totals[4],
        totals[5],
        totals[6],
        totals[7],
        totals[8],
        totals[9],
        totals[10],
        totals[11],
    )


def solution(mesh):
    in_specs = (
        P("wide", "narrow", None, None),
        P("wide"),
        P(("wide", "narrow"), None, None, None),
        P(),
        P(),
        P(),
        P(),
        P(),
        P(),
        P(),
        P(),
        P(),
        P(),
        P(),
        P(),
    )
    out_specs = (
        P(("wide", "narrow"), None, None, None),
        P("wide", "narrow", None, None),
        P(),
        P(),
        P(),
        P(),
        P(),
        P(),
        P(),
        P(),
        P(),
        P(),
        P(),
        P(),
    )
    return jax.shard_map(shards, mesh=mesh, in_specs=in_specs, out_specs=out_specs, check_vma=False)
```

profile of v0, /device:TPU:0, one launch (start us, length us, event | category | flops | bytes accessed | tf_op | source)
XLA Modules:
  0.0 1774.4 jit_solution(31865291041044090)
XLA Ops:
  66.4 10.9 reshape.293
  77.3 8.4 copy.84
  85.8 133.5 %all-gather.2.cloned.1.call-done = bf16[16,32,32,768]{3,2,1,0:T(8,128)(2,1)} async-done(((bf16[16,8,32,768]{3,2,1,0:T(8,128)(2,1)}), bf16[16,32,32,768]{3,2,1,0:T(8,128)(2,1)}) %all-gather.2.cloned.1.call-update) | async-done | bytes 25165840 | tf_op jit(solution)/shard_map/all_gather | solution.py:164
  219.3 19.0 %fusion.96 = (bf16[16,32,32,384]{3,2,1,0:T(8,128)(2,1)}, bf16[16,32,32,384]{3,2,1,0:T(8,128)(2,1)}) fusion(bf16[16,32,32,768]{3,2,1,0:T(8,128)(2,1)} %all-gather.2.cloned.1.call-done), kind=kLoop, calls=%fused_computation.245 | loop fusion | bytes 50331648 | tf_op jit(solution)/shard_map/slice | solution.py:167
  238.2 38.1 %reshape.295 = bf16[16,16,2,16,2,6,64]{6,5,4,3,2,1,0:T(8,128)(2,1)} reshape(bf16[16,32,32,384]{3,2,1,0:T(8,128)(2,1)} %get-tuple-element.82) | data formatting | bytes 25165824 | tf_op jit(solution)/shard_map/reshape | solution.py:88
  276.4 19.8 %copy.85 = bf16[16,2,2,6,16,16,64]{6,5,4,3,2,1,0:T(8,128)(2,1)} copy(bf16[16,2,2,6,16,16,64]{6,3,2,5,1,4,0:T(8,128)(2,1)} %bitcast.172) | data formatting | bytes 25165824 | tf_op jit(solution)/shard_map/transpose | solution.py:89
  296.2 27.0 %multiply_reduce_fusion.1 = (f32[16,4,6,64]{3,2,1,0:T(8,128)S(1)}, f32[16,4,6,64,256]{4,3,2,1,0:T(8,128)}) fusion(bf16[16,4,6,64,64]{4,3,2,1,0:T(8,128)(2,1)} %bitcast.180, bf16[16,4,6,256,64]{4,3,2,1,0:T(8,128)(2,1)} %bitcast.170), kind=kOutput, calls=%fused_computation.63 | convolution fusion | flops 817864704 | bytes 40992768 | tf_op jit(solution)/shard_map/bghqe,bghke->bghqk/dot_general | solution.py:122
  323.2 12.0 exponential_reduce_fusion
  335.3 38.2 %reshape.297 = bf16[16,16,2,16,2,6,64]{6,5,4,3,2,1,0:T(8,128)(2,1)} reshape(bf16[16,32,32,384]{3,2,1,0:T(8,128)(2,1)} %get-tuple-element.83) | data formatting | bytes 25165824 | tf_op jit(solution)/shard_map/reshape | solution.py:88
  373.5 19.8 %copy.87 = bf16[16,2,2,6,16,16,64]{6,5,4,3,2,1,0:T(8,128)(2,1)} copy(bf16[16,2,2,6,16,16,64]{6,3,2,5,1,4,0:T(8,128)(2,1)} %bitcast.173) | data formatting | bytes 25165824 | tf_op jit(solution)/shard_map/transpose | solution.py:89
  393.4 22.2 %convolution_convert_fusion.2 = bf16[16,4,6,64,64]{4,3,2,1,0:T(8,128)(2,1)} fusion(bf16[16,4,6,256,64]{4,3,2,1,0:T(8,128)(2,1)} %bitcast.168, f32[16,4,6,64,256]{4,3,2,1,0:T(8,128)} %get-tuple-element.105, f32[16,4,6,64]{3,2,1,0:T(8,128)S(1)} %log_add_fusion), kind=kOutput, calls=%fused_computation.160 | convolution fusion | flops 825753600 | bytes 40992768 | tf_op jit(solution)/shard_map/bghqk,bghke->bghqe/dot_general | solution.py:173
  415.6 15.2 copy.132
  430.8 11.6 convert_element_type.482
  453.4 8.9 add_convert_fusion
  480.9 8.9 copy.94
  489.8 8.5 reshape.299
  498.3 15.1 select_maximum_fusion.2
  513.4 52.4 %fusion.8 = f32[16,8,32,1536]{3,2,1,0:T(8,128)} fusion(bf16[16,8,32,1536]{3,2,1,0:T(8,128)(2,1)} %copy-done.5, bf16[16,1,32,1536]{3,2,1,0:T(8,128)(2,1)} %collective-permute-done.3, bf16[16,1,32,1536]{3,2,1,0:T(8,128)(2,1)} %collective-permute-done.2, f32[1536]{0:T(1024)S(1)} %get-tuple-element.51, f32[1536]{0:T(1024)S(1)} %get-tuple-element.52, ...), kind=kLoop, calls=%fused_computation.31 | loop fusion | flops 176160768 | bytes 116447232 | tf_op jit(solution)/shard_map/add | solution.py:58
  565.8 64.6 %fusion.22 = (f32[1536]{0:T(1024)}, f32[1536]{0:T(1024)}, f32[1536]{0:T(1024)}, f32[1536]{0:T(1024)}, f32[1536]{0:T(1024)}, /*index=5*/f32[1536]{0:T(1024)}, f32...) fusion(bf16[16,10,34,1536]{3,2,1,0:T(8,128)(2,1)} %select_maximum_fusion.2, ...), kind=kOutput, calls=%fused_computation.45 | convolution fusion | flops 5149542912 | bytes 136525824 | tf_op jit(solution)/shard_map/brwd,fd->brwf/dot_general | solution.py:211
  641.0 20.7 %select_maximum_fusion = bf16[16,10,34,1536]{3,2,1,0:T(8,128)(2,1)} fusion(bf16[16,1,32,1536]{3,2,1,0:T(8,128)(2,1)S(1)} %collective-permute-done.5, bf16[16,8,32,1536]{3,2,1,0:T(8,128)(2,1)} %get-tuple-element.112, bf16[16,1,32,1536]{3,2,1,0:T(8,128)(2,1)S(1)} %collective-permute-done.4), kind=kLoop, calls=%fused_computation.74 | loop fusion | flops 100270080 | bytes 32440320 | tf_op jit(solution)/shard_map/concatenate | solution.py:21
  661.7 50.8 %convert_reduce_fusion = (f32[1536]{0:T(1024)}, bf16[16,8,32,1536]{3,2,1,0:T(8,128)(2,1)}) fusion(f32[1536]{0:T(1024)S(1)} %get-tuple-element.51, bf16[16,10,34,1536]{3,2,1,0:T(8,128)(2,1)} %select_maximum_fusion, f32[1536]{0:T(1024)S(1)} %get-tuple-element.52, bf16[16,8,32,1536]{3,2,1,0:T(8,128)(2,1)} %get-tuple-element.112, ...), kind=kLoop, calls=%fused_computation.55 | loop fusion | flops 195033600 | bytes 103870464 | tf_op jit(solution)/shard_map/reduce_sum | solution.py:222
  712.5 11.4 multiply_reduce_fusion.5
  730.3 19.9 %multiply_reduce_fusion.2 = (f32[16,384]{1,0:T(8,128)}, bf16[16,8,32,384]{3,2,1,0:T(8,128)(2,1)}, f32[16,384]{1,0:T(8,128)}, f32[16,8,32,384]{3,2,1,0:T(8,128)S(1)}) fusion(f32[16,8,32,384]{3,2,1,0:T(8,128)} %reshape.299, f32[384]{0:T(512)S(1)} %convert_element_type.514, f32[16,8,32,384]{3,2,1,0:T(8,128)} %copy-done.6, f32[16,384]{1,0:T(8,128)S(1)} %copy-done.61, ...), kind=kOutput, calls=%fused_computation.143 | convolution fusion | flops 4913614848 | bytes 61113856 | tf_op jit(solution)/shard_map/dot_general | solution.py:187
  756.7 10.6 reshape.300
  775.0 28.2 %multiply_reduce_fusion = (f32[16,4,6,64]{3,2,1,0:T(8,128)S(1)}, f32[16,4,6,64,256]{4,3,2,1,0:T(8,128)}) fusion(f32[16,4,6,64,256]{4,3,2,1,0:T(8,128)} %get-tuple-element.105, f32[16,4,6,64]{3,2,1,0:T(8,128)S(1)} %copy-done.15, bf16[16,4,6,64,64]{4,3,2,1,0:T(8,128)(2,1)} %bitcast.178, bf16[16,4,6,256,64]{4,3,2,1,0:T(8,128)(2,1)} %bitcast.169), kind=kOutput, calls=%fused_computation.58 | convolution fusion | flops 830447616 | bytes 66256896 | tf_op jit(solution)/shard_map/bghqe,bghke->bghqk/dot_general | solution.py:241
  803.2 18.2 %convolution_convert_fusion.1 = bf16[16,4,6,256,64]{3,4,2,1,0:T(8,128)(2,1)} fusion(bf16[16,4,6,64,64]{4,3,2,1,0:T(8,128)(2,1)} %bitcast.179, f32[16,4,6,64,256]{4,3,2,1,0:T(8,128)} %get-tuple-element.105, f32[16,4,6,64]{3,2,1,0:T(8,128)S(1)} %copy-done.15), kind=kOutput, calls=%fused_computation.111 | convolution fusion | flops 830472192 | bytes 40992768 | tf_op jit(solution)/shard_map/bghqk,bghqe->bghke/dot_general | solution.py:244
  821.4 21.7 %multiply_convert_fusion.1 = bf16[16,4,6,64,256]{4,3,2,1,0:T(8,128)(2,1)} fusion(f32[16,4,6,64,256]{4,3,2,1,0:T(8,128)} %get-tuple-element.110, f32[16,4,6,64,256]{4,3,2,1,0:T(8,128)} %get-tuple-element.105, f32[16,4,6,64]{3,2,1,0:T(8,128)S(1)} %get-tuple-element.109, f32[16,4,6,64]{3,2,1,0:T(8,128)S(1)} %copy-done.15), kind=kLoop, calls=%fused_computation.57 | loop fusion | flops 31457280 | bytes 63111168 | tf_op jit(solution)/shard_map/convert_element_type | solution.py:248
  843.1 10.9 multiply_convert_fusion
  854.0 22.9 %copy.100 = bf16[16,4,6,256,64]{4,3,2,1,0:T(8,128)(2,1)} copy(bf16[16,4,6,256,64]{3,4,2,1,0:T(8,128)(2,1)} %multiply_convert_fusion) | data formatting | bytes 25165824 | tf_op jit(solution)/shard_map/convert.30
  876.9 36.9 %copy.101 = bf16[16,16,2,16,2,6,64]{6,5,4,3,2,1,0:T(8,128)(2,1)} copy(bf16[16,16,2,16,2,6,64]{6,3,1,5,4,2,0:T(8,128)(2,1)} %bitcast.175) | data formatting | bytes 25165824 | tf_op jit(solution)/shard_map/transpose | solution.py:98
  913.8 40.4 %reshape.305 = bf16[16,32,32,384]{3,2,1,0:T(8,128)(2,1)} reshape(bf16[16,16,2,16,2,6,64]{6,5,4,3,2,1,0:T(8,128)(2,1)} %copy.101) | data formatting | bytes 25165824 | tf_op jit(solution)/shard_map/reshape | solution.py:99
  954.3 22.9 %copy.103 = bf16[16,4,6,256,64]{4,3,2,1,0:T(8,128)(2,1)} copy(bf16[16,4,6,256,64]{3,4,2,1,0:T(8,128)(2,1)} %convolution_convert_fusion.1) | data formatting | bytes 25165824 | tf_op jit(solution)/shard_map/convert.27
  977.2 36.9 %copy.104 = bf16[16,16,2,16,2,6,64]{6,5,4,3,2,1,0:T(8,128)(2,1)} copy(bf16[16,16,2,16,2,6,64]{6,3,1,5,4,2,0:T(8,128)(2,1)} %bitcast.176) | data formatting | bytes 25165824 | tf_op jit(solution)/shard_map/transpose | solution.py:98
  1014.1 40.9 %reshape.307 = bf16[16,32,32,384]{3,2,1,0:T(8,128)(2,1)} reshape(bf16[16,16,2,16,2,6,64]{6,5,4,3,2,1,0:T(8,128)(2,1)} %copy.104) | data formatting | bytes 25165824 | tf_op jit(solution)/shard_map/reshape | solution.py:99
  1054.9 20.9 %pad_maximum_fusion = bf16[16,32,32,768]{3,2,1,0:T(8,128)(2,1)} fusion(bf16[16,32,32,384]{3,2,1,0:T(8,128)(2,1)} %reshape.307, bf16[16,32,32,384]{3,2,1,0:T(8,128)(2,1)} %reshape.305), kind=kLoop, calls=%fused_computation.54 | loop fusion | flops 50331648 | bytes 50331648 | tf_op jit(solution)/shard_map/concatenate | solution.py:256
  1075.8 12.5 copy.123
  1088.3 15.7 copy.125
  1107.3 17.7 convolution_bitcast_fusion.1
  1148.0 20.3 %multiply_convert_fusion.3 = bf16[16,4,6,64,64]{4,3,2,1,0:T(8,128)(2,1)} fusion(bf16[16,4,6,64,256]{4,3,2,1,0:T(8,128)(2,1)} %multiply_convert_fusion.1, bf16[16,4,6,256,64]{4,3,2,1,0:T(8,128)(2,1)} %bitcast.171), kind=kOutput, calls=%fused_computation.87 | convolution fusion | flops 808452096 | bytes 28311552 | tf_op jit(solution)/shard_map/bghqk,bghke->bghqe/dot_general | solution.py:250
  1168.3 15.2 copy.131
  1183.5 11.4 reshape.303
  1219.2 82.2 %reduce-scatter.5.cloned.1.call-done = bf16[8,393216]{1,0:T(8,128)(2,1)} async-done(((bf16[32,393216]{1,0:T(8,128)(2,1)}), bf16[8,393216]{1,0:T(8,128)(2,1)}) %reduce-scatter.5.cloned.1.call-update) | async-done | bytes 6291472
  1309.1 21.1 %fusion.59 = (f32[384]{0:T(512)S(1)}, f32[384]{0:T(512)S(1)}, f32[384]{0:T(512)S(1)}, f32[384]{0:T(512)S(1)}, f32[384]{0:T(512)S(1)}, /*index=5*/f32[384]{0:T(51...) fusion(bf16[16,10,34,384]{3,2,1,0:T(8,128)(2,1)} %copy-done.4, ...), kind=kOutput, calls=%fused_computation.131 | convolution fusion | flops 3672632832 | bytes 36288000 | tf_op jit(solution)/shard_map/brwe,de->brwd/dot_general | solution.py:272
  1334.7 10.1 convolution_bitcast_fusion.3
  1348.6 9.5 fusion.53
  1370.7 24.3 %all_to_all.36 = bf16[16,4,16,768]{3,2,1,0:T(8,128)(2,1)S(1)} all-to-all(bf16[16,4,16,768]{3,2,1,0:T(8,128)(2,1)S(1)} %add_convert_fusion.3), channel_id=1, replica_groups=mesh['wide'=8,'narrow'=4] {'narrow'}, dimensions={0} | all-to-all | bytes 3145728 | tf_op jit(solution)/shard_map/all_to_all | solution.py:196
  1400.7 89.1 %all-reduce.9.cloned.1.call-done = (f32[2304]{0:T(1024)}, f32[3,3,384]{2,1,0:T(4,128)}, f32[1536]{0:T(1024)}, f32[3,3,1536]{2,1,0:T(4,128)}, f32[384]{0:T(512)}, /*index=5*/f32[768]{0:T(1024)}) async-done(((f32[2304]{0:T(1024)}, f32[3,3,384]{2,1,0:T(4,128)}, f32[1536]{0:T(1024)}, f32[3,3,1536]{2,1,0:T(4,128)}, f32[384]{0:T(512)}, /*index=5*/f32[768]{0:T(1024)}), (f32[2304]{0:T(1024)}, ...) | async-done | bytes 89104 | tf_op jit(solution)/shard_map/psum | solution.py:293
  1489.8 260.7 %all-reduce.11.cloned.1.call-done = (f32[256,2304]{1,0:T(8,128)}, f32[384,1152]{1,0:T(8,128)}, f32[384,384]{1,0:T(8,128)}, f32[384,1536]{1,0:T(8,128)}, f32[1536,384]{1,0:T(8,128)}, /*index=5*/f32[1536,768]{1,0:T(8,128)}) async-done(((f32[256,2304]{1,0:T(8,128)}, f32[384,1152]{1,0:T(8,128)}, f32[384,384]{1,0:T(8,128)}, f32[384,1536]{1,0:T(8,128)}, f32[1536,384]{1,0:T(8,128)}, ...) | async-done | bytes 14155792 | tf_op jit(solution)/shard_map/psum | solution.py:293
  (358 shorter events, 220.4 us)
Async XLA Ops:
  7.2 468.1 %copy-start = (bf16[1536,768]{1,0:T(8,128)(2,1)S(1)}, bf16[1536,768]{1,0:T(8,128)(2,1)}, u32[]{:S(2)}) copy-start(bf16[1536,768]{1,0:T(8,128)(2,1)} %param.28) | copy-start | bytes 7077892
  7.2 212.1 %all-gather.2.cloned.1.call-start = ((), (), s32[]{:S(2)}) async-start(), calls=%async_computation.3 | async-start | bytes 31457280 | tf_op jit(solution)/shard_map/all_gather | solution.py:164
  14.8 14.2 copy-start.30
  15.0 14.1 copy-start.54
  15.0 14.1 copy-start.56
  16.3 12.7 copy-start.32
  18.2 19.0 %copy-start.8 = (bf16[16,8,32,384]{3,2,1,0:T(8,128)(2,1)}, bf16[16,8,32,384]{3,2,1,0:T(8,128)(2,1)S(1)}, u32[]{:S(2)}) copy-start(bf16[16,8,32,384]{3,2,1,0:T(8,128)(2,1)S(1)} %fusion.41) | copy-start | bytes 9437188
  18.4 3.8 collective-permute-start
  20.8 5.7 collective-permute-start.1
  22.1 15.2 copy-start.66
  22.1 15.2 copy-start.68
  22.1 15.2 copy-start.70
  22.1 15.2 copy-start.72
  22.2 15.2 copy-start.74
  22.2 15.2 copy-start.76
  22.2 15.2 copy-start.78
  22.2 15.2 copy-start.80
  22.2 15.2 copy-start.82
  22.2 15.1 copy-start.21
  54.6 419.1 %all-to-all-start.1 = ((bf16[4,16,16,768]{3,2,0,1:T(8,128)(2,1)}), bf16[4,16,16,768]{3,2,0,1:T(8,128)(2,1)}, u32[]{:S(2)}, u32[]{:S(2)}) async-start(bf16[4,16,16,768]{3,2,0,1:T(8,128)(2,1)} %copy.92), calls=%async_computation.1 | async-start | bytes 3145728 | tf_op jit(solution)/shard_map/all_to_all | solution.py:197
  61.8 1239.6 %reduce-scatter.5.cloned.1.call-start = ((), (), s32[]{:S(2)}) async-start(), calls=%async_computation.4 | async-start | bytes 31457280
  335.3 58.1 %copy-start.14 = (f32[16,4,6,64]{3,2,1,0:T(8,128)}, f32[16,4,6,64]{3,2,1,0:T(8,128)S(1)}, u32[]{:S(2)}) copy-start(f32[16,4,6,64]{3,2,1,0:T(8,128)S(1)} %log_add_fusion) | copy-start | bytes 294916
  430.8 11.6 copy-start.28
  430.8 11.6 copy-start.45
  450.7 11.6 copy-start.34
  468.9 29.4 %collective-permute-start.2 = (bf16[16,1,32,1536]{3,2,1,0:T(8,128)(2,1)}, bf16[16,1,32,1536]{3,2,1,0:T(8,128)(2,1)}, u32[]{:S(2)}, u32[]{:S(2)}) collective-permute-start(bf16[16,1,32,1536]{3,2,1,0:T(8,128)(2,1)} %get-tuple-element.86), channel_id=1, source_target_pairs={{0,1},{1,2},{2,3},{4,5},{5,6},{6,7},{8,9},{9,10},{10,11},{12,13},{... | collective-permute-start | bytes 4718600 | tf_op jit(solution)/shard_map/ppermute | solution.py:17
  472.2 26.1 %collective-permute-start.3 = (bf16[16,1,32,1536]{3,2,1,0:T(8,128)(2,1)}, bf16[16,1,32,1536]{3,2,1,0:T(8,128)(2,1)}, u32[]{:S(2)}, u32[]{:S(2)}) collective-permute-start(bf16[16,1,32,1536]{3,2,1,0:T(8,128)(2,1)} %get-tuple-element.87), channel_id=1, source_target_pairs={{1,0},{2,1},{3,2},{5,4},{6,5},{7,6},{9,8},{10,9},{11,10},{13,12},{... | collective-permute-start | bytes 4718600 | tf_op jit(solution)/shard_map/ppermute | solution.py:20
  513.4 52.4 %copy-start.100 = (bf16[1536,384]{1,0:T(8,128)(2,1)S(1)}, bf16[1536,384]{1,0:T(8,128)(2,1)}, u32[]{:S(2)}) copy-start(bf16[1536,384]{1,0:T(8,128)(2,1)} %param.26) | copy-start | bytes 3538948
  632.6 6.0 collective-permute-start.4
  635.7 5.3 collective-permute-start.5
  661.7 50.8 %copy-start.35 = (f32[16,8,32]{2,1,0:T(8,128)S(1)}, f32[16,8,32]{2,1,0:T(8,128)}, u32[]{:S(2)}) copy-start(f32[16,8,32]{2,1,0:T(8,128)} %copy-done.34) | copy-start | bytes 49156
  661.7 50.8 %copy-start.49 = (f32[16,384]{1,0:T(8,128)S(1)}, f32[16,384]{1,0:T(8,128)}, u32[]{:S(2)}) copy-start(f32[16,384]{1,0:T(8,128)} %get-tuple-element.98) | copy-start | bytes 73732
  712.5 11.4 copy-start.43
  730.2 22.7 %copy-start.29 = (bf16[384,384]{1,0:T(8,128)(2,1)S(1)}, bf16[384,384]{1,0:T(8,128)(2,1)}, u32[]{:S(2)}) copy-start(bf16[384,384]{1,0:T(8,128)(2,1)} %param.22) | copy-start | bytes 884740
  730.2 22.7 %copy-start.46 = (f32[16,384]{1,0:T(8,128)S(1)}, f32[16,384]{1,0:T(8,128)}, u32[]{:S(2)}) copy-start(f32[16,384]{1,0:T(8,128)} %get-tuple-element.101) | copy-start | bytes 73732
  1104.1 385.7 %all-reduce.9.cloned.1.call-start = ((), (), s32[]{:S(2)}) async-start(), calls=%async_computation.5 | async-start | bytes 237568 | tf_op jit(solution)/shard_map/psum | solution.py:293
  1183.5 15.4 copy-start.47
  1331.4 14.4 collective-permute-start.6
  1333.2 12.6 copy-start.12
  1333.2 12.6 collective-permute-start.7
  1362.7 387.7 %all-reduce.11.cloned.1.call-start = ((), (), s32[]{:S(2)}) async-start(), calls=%async_computation.6 | async-start | bytes 28311552 | tf_op jit(solution)/shard_map/psum | solution.py:293
  1366.0 30.3 %slice-start.2 = ((s8[6291456]{0:T(1024)(128)(4,1)}), s8[4194304]{0:T(1024)(128)(4,1)S(1)}, s32[]{:S(2)}) async-start(s8[6291456]{0:T(1024)(128)(4,1)} %bitcast.184), calls=%async_computation.9 | async-start | bytes 8388608
  1366.0 30.3 %slice-start.4 = ((s8[6291456]{0:T(1024)(128)(4,1)}), s8[4194304]{0:T(1024)(128)(4,1)S(1)}, s32[]{:S(2)}) async-start(s8[6291456]{0:T(1024)(128)(4,1)} %bitcast.193), calls=%async_computation.11 | async-start | bytes 8388608
  1366.0 30.3 %slice-start.3 = ((s8[6291456]{0:T(1024)(128)(4,1)}), s8[2097152]{0:T(1024)(128)(4,1)S(1)}, s32[]{:S(2)}) async-start(s8[6291456]{0:T(1024)(128)(4,1)} %bitcast.184), calls=%async_computation.10 | async-start | bytes 4194304
  1366.0 30.3 %slice-start.5 = ((s8[6291456]{0:T(1024)(128)(4,1)}), s8[2097152]{0:T(1024)(128)(4,1)S(1)}, s32[]{:S(2)}) async-start(s8[6291456]{0:T(1024)(128)(4,1)} %bitcast.193), calls=%async_computation.12 | async-start | bytes 4194304
  1370.7 25.6 %copy-start.3 = (bf16[16,8,32,384]{3,2,1,0:T(8,128)(2,1)S(1)}, bf16[16,8,32,384]{3,2,1,0:T(8,128)(2,1)}, u32[]{:S(2)}) copy-start(bf16[16,8,32,384]{3,2,1,0:T(8,128)(2,1)} %param.15) | copy-start | bytes 9437188
  1750.4 11.8 copy-start.58
  1750.4 12.4 copy-start.19
  (79 other events, 421.5 us)
Sparse Core Ops, SparseCore 0:
  52.0 167.2 all-gather.1
  1104.2 197.1 reduce-scatter.4
  1362.8 126.8 all-reduce.8
  1498.3 252.0 all-reduce.10
where the time goes:
time: 1790 us; the launch traced here: 1770 us
  waiting for transfers between devices  574 us (32%)
  local copies, waits for them, and re-layouts  561 us (31%)
  matrix products  329 us (18%)
  other arithmetic  247 us (14%)
  blocking collectives  24.3 us (1%)
  starting transfers between devices  23.5 us (1%)
    psum x2, waiting for transfers between devices, shards(): lax.psum((grad_ada_weight, grad_ada_bias, grad_conv_attn, grad_qkv_weight...  350 us
    all_gather x1, waiting for transfers between devices, shards(): pair_all = lax.all_gather(pair_own, 'narrow', axis=1, tiled=True)  133 us
    reshape x4, local copies, waits for them, and re-layouts, to_groups(): values.reshape(batch_size, row_count // 2, 2, col_count // 2, 2, head_cou...  97.9 us
    reshape x3, local copies, waits for them, and re-layouts, from_groups(): shaped.reshape(batch_size, row_count, col_count, head_count * head_size)  92.7 us
    unnamed x5, waiting for transfers between devices  82.3 us
    transpose x2, local copies, waits for them, and re-layouts, from_groups(): shaped = shaped.transpose(0, 4, 1, 5, 2, 3, 6)  73.8 us
    unnamed x250, local copies, waits for them, and re-layouts  73.6 us
    dot_general x1, matrix products, shards(): jnp.einsum('brwd,fd->brwf', grad_ffn_out, fc2_weight, preferred_element_t...  64.6 us
  transfers between devices with their start and end apart: 13, of which 7 were waited for; matrix products, arithmetic and copies ran while one was open for 24% of the time, Pallas kernels for 0%

commit v1 on v0

--- a/solution.py
+++ b/solution.py
@@ -291,21 +291,24 @@
     grad_ada_weight = jnp.dot(cond_all.astype(jnp.float32).T, grad_modulation, precision=HIGH)
     grad_ada_bias = jnp.sum(grad_modulation, axis=0)
     totals = lax.psum(
-        (
-            grad_ada_weight,
-            grad_ada_bias,
-            grad_conv_attn,
-            grad_qkv_weight,
-            grad_proj_weight,
-            grad_fc1_weight,
-            grad_fc1_bias,
-            grad_conv_ffn,
-            grad_fc2_weight,
-            grad_fc2_bias,
-            grad_down_weight,
-            grad_down_bias,
+        lax.psum(
+            (
+                grad_ada_weight,
+                grad_ada_bias,
+                grad_conv_attn,
+                grad_qkv_weight,
+                grad_proj_weight,
+                grad_fc1_weight,
+                grad_fc1_bias,
+                grad_conv_ffn,
+                grad_fc2_weight,
+                grad_fc2_bias,
+                grad_down_weight,
+                grad_down_bias,
+            ),
+            "narrow",
         ),
-        ("wide", "narrow"),
+        "wide",
     )
     return (
         result,

time: 1790 us -> 2210 us (1.23)
  waiting for transfers between devices: 574 us -> 997 us
    psum x0 -> x2, waiting for transfers between devices: none -> 489 us  [shards(): lax.psum(lax.psum((grad_ada_weight, grad_ada_bias, grad_conv_attn, grad_q...]
    psum x2, waiting for transfers between devices: 350 us -> 284 us  [shards(): lax.psum((grad_ada_weight, grad_ada_bias, grad_conv_attn, grad_qkv_weight...]
    unnamed x5 -> x7, waiting for transfers between devices: 82.3 us -> 82.3 us
  transfers between devices with their start and end apart: 13 -> 15, of which waited for: 7 -> 9; matrix products, arithmetic and copies ran while one was open for 24% -> 20% of each run, Pallas kernels for 0% -> 0%
where the time goes in v1:
time: 2210 us; the launch traced here: 2200 us
  waiting for transfers between devices  997 us (45%)
  local copies, waits for them, and re-layouts  561 us (25%)
  matrix products  329 us (15%)
  other arithmetic  247 us (11%)
  starting transfers between devices  23.6 us (1%)
  blocking collectives  22.8 us (1%)
    psum x2, waiting for transfers between devices, shards(): lax.psum(lax.psum((grad_ada_weight, grad_ada_bias, grad_conv_attn, grad_q...  489 us
    psum x2, waiting for transfers between devices, shards(): lax.psum((grad_ada_weight, grad_ada_bias, grad_conv_attn, grad_qkv_weight...  284 us
    all_gather x1, waiting for transfers between devices, shards(): pair_all = lax.all_gather(pair_own, 'narrow', axis=1, tiled=True)  133 us
    reshape x4, local copies, waits for them, and re-layouts, to_groups(): values.reshape(batch_size, row_count // 2, 2, col_count // 2, 2, head_cou...  97.9 us
    reshape x3, local copies, waits for them, and re-layouts, from_groups(): shaped.reshape(batch_size, row_count, col_count, head_count * head_size)  92.7 us
    unnamed x7, waiting for transfers between devices  82.3 us
    transpose x2, local copies, waits for them, and re-layouts, from_groups(): shaped = shaped.transpose(0, 4, 1, 5, 2, 3, 6)  73.8 us
    unnamed x250, local copies, waits for them, and re-layouts  73.6 us
  transfers between devices with their start and end apart: 15, of which 9 were waited for; matrix products, arithmetic and copies ran while one was open for 20% of the time, Pallas kernels for 0%

profile of v1, /device:TPU:0, one launch (start us, length us, event | category | flops | bytes accessed | tf_op | source)
XLA Modules:
  0.0 2196.9 jit_solution(17467162345358427233)
XLA Ops:
  66.4 10.9 reshape.293
  85.8 133.5 %all-gather.2.cloned.1.call-done = bf16[16,32,32,768]{3,2,1,0:T(8,128)(2,1)} async-done(((bf16[16,8,32,768]{3,2,1,0:T(8,128)(2,1)}), bf16[16,32,32,768]{3,2,1,0:T(8,128)(2,1)}) %all-gather.2.cloned.1.call-update) | async-done | bytes 25165840 | tf_op jit(solution)/shard_map/all_gather | solution.py:164
  219.3 19.0 fusion.96
  238.2 38.1 %reshape.295 = bf16[16,16,2,16,2,6,64]{6,5,4,3,2,1,0:T(8,128)(2,1)} reshape(bf16[16,32,32,384]{3,2,1,0:T(8,128)(2,1)} %get-tuple-element.94) | data formatting | bytes 25165824 | tf_op jit(solution)/shard_map/reshape | solution.py:88
  276.4 19.8 copy.85
  296.2 27.0 %multiply_reduce_fusion.1 = (f32[16,4,6,64]{3,2,1,0:T(8,128)S(1)}, f32[16,4,6,64,256]{4,3,2,1,0:T(8,128)}) fusion(bf16[16,4,6,64,64]{4,3,2,1,0:T(8,128)(2,1)} %bitcast.180, bf16[16,4,6,256,64]{4,3,2,1,0:T(8,128)(2,1)} %bitcast.170), kind=kOutput, calls=%fused_computation.63 | convolution fusion | flops 817864704 | bytes 40992768 | tf_op jit(solution)/shard_map/bghqe,bghke->bghqk/dot_general | solution.py:122
  323.2 12.0 exponential_reduce_fusion
  335.3 38.2 %reshape.297 = bf16[16,16,2,16,2,6,64]{6,5,4,3,2,1,0:T(8,128)(2,1)} reshape(bf16[16,32,32,384]{3,2,1,0:T(8,128)(2,1)} %get-tuple-element.95) | data formatting | bytes 25165824 | tf_op jit(solution)/shard_map/reshape | solution.py:88
  373.5 19.8 copy.87
  393.4 22.2 %convolution_convert_fusion.2 = bf16[16,4,6,64,64]{4,3,2,1,0:T(8,128)(2,1)} fusion(bf16[16,4,6,256,64]{4,3,2,1,0:T(8,128)(2,1)} %bitcast.168, f32[16,4,6,64,256]{4,3,2,1,0:T(8,128)} %get-tuple-element.117, f32[16,4,6,64]{3,2,1,0:T(8,128)S(1)} %log_add_fusion), kind=kOutput, calls=%fused_computation.160 | convolution fusion | flops 825753600 | bytes 40992768 | tf_op jit(solution)/shard_map/bghqk,bghke->bghqe/dot_general | solution.py:173
  415.6 15.2 copy.132
  430.8 11.6 convert_element_type.482
  453.4 8.9 add_convert_fusion
  480.9 8.9 copy.94
  498.3 15.1 select_maximum_fusion.2
  513.4 52.4 %fusion.8 = f32[16,8,32,1536]{3,2,1,0:T(8,128)} fusion(bf16[16,8,32,1536]{3,2,1,0:T(8,128)(2,1)} %copy-done.5, bf16[16,1,32,1536]{3,2,1,0:T(8,128)(2,1)} %collective-permute-done.3, bf16[16,1,32,1536]{3,2,1,0:T(8,128)(2,1)} %collective-permute-done.2, f32[1536]{0:T(1024)S(1)} %get-tuple-element.51, f32[1536]{0:T(1024)S(1)} %get-tuple-element.52, ...), kind=kLoop, calls=%fused_computation.31 | loop fusion | flops 176160768 | bytes 116447232 | tf_op jit(solution)/shard_map/add | solution.py:58
  565.8 64.6 %fusion.22 = (f32[1536]{0:T(1024)}, f32[1536]{0:T(1024)}, f32[1536]{0:T(1024)}, f32[1536]{0:T(1024)}, f32[1536]{0:T(1024)}, /*index=5*/f32[1536]{0:T(1024)}, f32...) fusion(bf16[16,10,34,1536]{3,2,1,0:T(8,128)(2,1)} %select_maximum_fusion.2, ...), kind=kOutput, calls=%fused_computation.45 | convolution fusion | flops 5149542912 | bytes 136525824 | tf_op jit(solution)/shard_map/brwd,fd->brwf/dot_general | solution.py:211
  641.0 20.7 select_maximum_fusion
  661.7 50.8 %convert_reduce_fusion = (f32[1536]{0:T(1024)}, bf16[16,8,32,1536]{3,2,1,0:T(8,128)(2,1)}) fusion(f32[1536]{0:T(1024)S(1)} %get-tuple-element.51, bf16[16,10,34,1536]{3,2,1,0:T(8,128)(2,1)} %select_maximum_fusion, f32[1536]{0:T(1024)S(1)} %get-tuple-element.52, bf16[16,8,32,1536]{3,2,1,0:T(8,128)(2,1)} %get-tuple-element.124, ...), kind=kLoop, calls=%fused_computation.55 | loop fusion | flops 195033600 | bytes 103870464 | tf_op jit(solution)/shard_map/reduce_sum | solution.py:222
  712.5 11.4 multiply_reduce_fusion.5
  730.3 19.9 multiply_reduce_fusion.2
  756.7 10.6 reshape.300
  775.0 28.2 %multiply_reduce_fusion = (f32[16,4,6,64]{3,2,1,0:T(8,128)S(1)}, f32[16,4,6,64,256]{4,3,2,1,0:T(8,128)}) fusion(f32[16,4,6,64,256]{4,3,2,1,0:T(8,128)} %get-tuple-element.117, f32[16,4,6,64]{3,2,1,0:T(8,128)S(1)} %copy-done.15, bf16[16,4,6,64,64]{4,3,2,1,0:T(8,128)(2,1)} %bitcast.178, bf16[16,4,6,256,64]{4,3,2,1,0:T(8,128)(2,1)} %bitcast.169), kind=kOutput, calls=%fused_computation.58 | convolution fusion | flops 830447616 | bytes 66256896 | tf_op jit(solution)/shard_map/bghqe,bghke->bghqk/dot_general | solution.py:241
  803.2 18.2 convolution_convert_fusion.1
  821.4 21.7 multiply_convert_fusion.1
  843.1 10.9 multiply_convert_fusion
  854.0 22.9 %copy.100 = bf16[16,4,6,256,64]{4,3,2,1,0:T(8,128)(2,1)} copy(bf16[16,4,6,256,64]{3,4,2,1,0:T(8,128)(2,1)} %multiply_convert_fusion) | data formatting | bytes 25165824 | tf_op jit(solution)/shard_map/convert.30
  876.9 36.9 %copy.101 = bf16[16,16,2,16,2,6,64]{6,5,4,3,2,1,0:T(8,128)(2,1)} copy(bf16[16,16,2,16,2,6,64]{6,3,1,5,4,2,0:T(8,128)(2,1)} %bitcast.175) | data formatting | bytes 25165824 | tf_op jit(solution)/shard_map/transpose | solution.py:98
  913.8 40.4 %reshape.305 = bf16[16,32,32,384]{3,2,1,0:T(8,128)(2,1)} reshape(bf16[16,16,2,16,2,6,64]{6,5,4,3,2,1,0:T(8,128)(2,1)} %copy.101) | data formatting | bytes 25165824 | tf_op jit(solution)/shard_map/reshape | solution.py:99
  954.3 22.9 %copy.103 = bf16[16,4,6,256,64]{4,3,2,1,0:T(8,128)(2,1)} copy(bf16[16,4,6,256,64]{3,4,2,1,0:T(8,128)(2,1)} %convolution_convert_fusion.1) | data formatting | bytes 25165824 | tf_op jit(solution)/shard_map/convert.27
  977.2 36.9 %copy.104 = bf16[16,16,2,16,2,6,64]{6,5,4,3,2,1,0:T(8,128)(2,1)} copy(bf16[16,16,2,16,2,6,64]{6,3,1,5,4,2,0:T(8,128)(2,1)} %bitcast.176) | data formatting | bytes 25165824 | tf_op jit(solution)/shard_map/transpose | solution.py:98
  1014.1 40.9 %reshape.307 = bf16[16,32,32,384]{3,2,1,0:T(8,128)(2,1)} reshape(bf16[16,16,2,16,2,6,64]{6,5,4,3,2,1,0:T(8,128)(2,1)} %copy.104) | data formatting | bytes 25165824 | tf_op jit(solution)/shard_map/reshape | solution.py:99
  1054.9 20.9 pad_maximum_fusion
  1075.8 12.5 copy.123
  1088.3 15.7 copy.125
  1107.3 17.7 convolution_bitcast_fusion.1
  1148.0 20.3 multiply_convert_fusion.3
  1168.3 15.2 copy.131
  1183.5 11.4 reshape.303
  1219.2 82.2 %reduce-scatter.5.cloned.1.call-done = bf16[8,393216]{1,0:T(8,128)(2,1)} async-done(((bf16[32,393216]{1,0:T(8,128)(2,1)}), bf16[8,393216]{1,0:T(8,128)(2,1)}) %reduce-scatter.5.cloned.1.call-update) | async-done | bytes 6291472
  1309.1 21.1 fusion.59
  1334.7 10.1 convolution_bitcast_fusion.3
  1348.6 9.5 fusion.53
  1365.4 31.2 %all-reduce.17.cloned.1.call-done = (f32[2304]{0:T(1024)}, f32[3,3,384]{2,1,0:T(4,128)}, f32[1536]{0:T(1024)}, f32[3,3,1536]{2,1,0:T(4,128)}, f32[384]{0:T(512)}, /*index=5*/f32[768]{0:T(1024)}) async-done(((f32[2304]{0:T(1024)}, f32[3,3,384]{2,1,0:T(4,128)}, f32[1536]{0:T(1024)}, f32[3,3,1536]{2,1,0:T(4,128)}, f32[384]{0:T(512)}, /*index=5*/f32[768]{0:T(1024)}), (f32[2304]{0:T(1024)}, ...) | async-done | bytes 89104 | tf_op jit(solution)/shard_map/psum | solution.py:294
  1396.6 252.7 %all-reduce.19.cloned.1.call-done = (f32[256,2304]{1,0:T(8,128)}, f32[384,1152]{1,0:T(8,128)}, f32[384,384]{1,0:T(8,128)}, f32[384,1536]{1,0:T(8,128)}, f32[1536,384]{1,0:T(8,128)}, /*index=5*/f32[1536,768]{1,0:T(8,128)}) async-done(((f32[256,2304]{1,0:T(8,128)}, f32[384,1152]{1,0:T(8,128)}, f32[384,384]{1,0:T(8,128)}, f32[384,1536]{1,0:T(8,128)}, f32[1536,384]{1,0:T(8,128)}, ...) | async-done | bytes 14155792 | tf_op jit(solution)/shard_map/psum | solution.py:294
  1654.7 22.8 %all_to_all.36 = bf16[16,4,16,768]{3,2,1,0:T(8,128)(2,1)S(1)} all-to-all(bf16[16,4,16,768]{3,2,1,0:T(8,128)(2,1)S(1)} %add_convert_fusion.3), channel_id=1, replica_groups=mesh['wide'=8,'narrow'=4] {'narrow'}, dimensions={0} | all-to-all | bytes 3145728 | tf_op jit(solution)/shard_map/all_to_all | solution.py:196
  1683.2 41.1 %all-reduce.13.cloned.1.call-done = (f32[2304]{0:T(1024)}, f32[3,3,384]{2,1,0:T(4,128)}, f32[1536]{0:T(1024)}, f32[3,3,1536]{2,1,0:T(4,128)}, f32[384]{0:T(512)}, /*index=5*/f32[768]{0:T(1024)}) async-done(((f32[2304]{0:T(1024)}, f32[3,3,384]{2,1,0:T(4,128)}, f32[1536]{0:T(1024)}, f32[3,3,1536]{2,1,0:T(4,128)}, f32[384]{0:T(512)}, /*index=5*/f32[768]{0:T(1024)}), (f32[2304]{0:T(1024)}, ...) | async-done | bytes 89104 | tf_op jit(solution)/shard_map/psum | solution.py:293
  1724.3 448.4 %all-reduce.15.cloned.1.call-done = (f32[256,2304]{1,0:T(8,128)}, f32[384,1152]{1,0:T(8,128)}, f32[384,384]{1,0:T(8,128)}, f32[384,1536]{1,0:T(8,128)}, f32[1536,384]{1,0:T(8,128)}, /*index=5*/f32[1536,768]{1,0:T(8,128)}) async-done(((f32[256,2304]{1,0:T(8,128)}, f32[384,1152]{1,0:T(8,128)}, f32[384,384]{1,0:T(8,128)}, f32[384,1536]{1,0:T(8,128)}, f32[1536,384]{1,0:T(8,128)}, ...) | async-done | bytes 14155792 | tf_op jit(solution)/shard_map/psum | solution.py:293
  (364 shorter events, 237.4 us)
Async XLA Ops:
  7.2 468.1 %copy-start = (bf16[1536,768]{1,0:T(8,128)(2,1)S(1)}, bf16[1536,768]{1,0:T(8,128)(2,1)}, u32[]{:S(2)}) copy-start(bf16[1536,768]{1,0:T(8,128)(2,1)} %param.28) | copy-start | bytes 7077892
  7.2 212.1 %all-gather.2.cloned.1.call-start = ((), (), s32[]{:S(2)}) async-start(), calls=%async_computation.3 | async-start | bytes 31457280 | tf_op jit(solution)/shard_map/all_gather | solution.py:164
  14.8 14.2 copy-start.30
  15.0 14.1 copy-start.54
  15.0 14.1 copy-start.56
  16.3 12.7 copy-start.32
  18.2 19.0 copy-start.8
  18.4 3.8 collective-permute-start
  20.8 5.7 collective-permute-start.1
  22.1 15.2 copy-start.66
  22.1 15.2 copy-start.68
  22.1 15.2 copy-start.70
  22.1 15.2 copy-start.72
  22.2 15.2 copy-start.74
  22.2 15.2 copy-start.76
  22.2 15.2 copy-start.78
  22.2 15.2 copy-start.80
  22.2 15.2 copy-start.82
  22.2 15.1 copy-start.21
  54.6 419.1 %all-to-all-start.1 = ((bf16[4,16,16,768]{3,2,0,1:T(8,128)(2,1)}), bf16[4,16,16,768]{3,2,0,1:T(8,128)(2,1)}, u32[]{:S(2)}, u32[]{:S(2)}) async-start(bf16[4,16,16,768]{3,2,0,1:T(8,128)(2,1)} %copy.92), calls=%async_computation.1 | async-start | bytes 3145728 | tf_op jit(solution)/shard_map/all_to_all | solution.py:197
  61.8 1239.6 %reduce-scatter.5.cloned.1.call-start = ((), (), s32[]{:S(2)}) async-start(), calls=%async_computation.4 | async-start | bytes 31457280
  335.3 58.1 %copy-start.14 = (f32[16,4,6,64]{3,2,1,0:T(8,128)}, f32[16,4,6,64]{3,2,1,0:T(8,128)S(1)}, u32[]{:S(2)}) copy-start(f32[16,4,6,64]{3,2,1,0:T(8,128)S(1)} %log_add_fusion) | copy-start | bytes 294916
  430.8 11.6 copy-start.45
  450.7 11.6 copy-start.34
  468.9 29.4 %collective-permute-start.2 = (bf16[16,1,32,1536]{3,2,1,0:T(8,128)(2,1)}, bf16[16,1,32,1536]{3,2,1,0:T(8,128)(2,1)}, u32[]{:S(2)}, u32[]{:S(2)}) collective-permute-start(bf16[16,1,32,1536]{3,2,1,0:T(8,128)(2,1)} %get-tuple-element.98), channel_id=1, source_target_pairs={{0,1},{1,2},{2,3},{4,5},{5,6},{6,7},{8,9},{9,10},{10,11},{12,13},{... | collective-permute-start | bytes 4718600 | tf_op jit(solution)/shard_map/ppermute | solution.py:17
  472.2 26.1 %collective-permute-start.3 = (bf16[16,1,32,1536]{3,2,1,0:T(8,128)(2,1)}, bf16[16,1,32,1536]{3,2,1,0:T(8,128)(2,1)}, u32[]{:S(2)}, u32[]{:S(2)}) collective-permute-start(bf16[16,1,32,1536]{3,2,1,0:T(8,128)(2,1)} %get-tuple-element.99), channel_id=1, source_target_pairs={{1,0},{2,1},{3,2},{5,4},{6,5},{7,6},{9,8},{10,9},{11,10},{13,12},{... | collective-permute-start | bytes 4718600 | tf_op jit(solution)/shard_map/ppermute | solution.py:20
  513.4 52.4 %copy-start.100 = (bf16[1536,384]{1,0:T(8,128)(2,1)S(1)}, bf16[1536,384]{1,0:T(8,128)(2,1)}, u32[]{:S(2)}) copy-start(bf16[1536,384]{1,0:T(8,128)(2,1)} %param.26) | copy-start | bytes 3538948
  632.6 6.0 collective-permute-start.4
  635.7 5.3 collective-permute-start.5
  661.7 50.8 %copy-start.35 = (f32[16,8,32]{2,1,0:T(8,128)S(1)}, f32[16,8,32]{2,1,0:T(8,128)}, u32[]{:S(2)}) copy-start(f32[16,8,32]{2,1,0:T(8,128)} %copy-done.34) | copy-start | bytes 49156
  661.7 50.8 %copy-start.49 = (f32[16,384]{1,0:T(8,128)S(1)}, f32[16,384]{1,0:T(8,128)}, u32[]{:S(2)}) copy-start(f32[16,384]{1,0:T(8,128)} %get-tuple-element.110) | copy-start | bytes 73732
  730.2 22.7 %copy-start.29 = (bf16[384,384]{1,0:T(8,128)(2,1)S(1)}, bf16[384,384]{1,0:T(8,128)(2,1)}, u32[]{:S(2)}) copy-start(bf16[384,384]{1,0:T(8,128)(2,1)} %param.22) | copy-start | bytes 884740
  730.2 22.7 %copy-start.46 = (f32[16,384]{1,0:T(8,128)S(1)}, f32[16,384]{1,0:T(8,128)}, u32[]{:S(2)}) copy-start(f32[16,384]{1,0:T(8,128)} %get-tuple-element.113) | copy-start | bytes 73732
  1104.1 292.5 %all-reduce.17.cloned.1.call-start = ((), (), s32[]{:S(2)}) async-start(), calls=%async_computation.7 | async-start | bytes 237568 | tf_op jit(solution)/shard_map/psum | solution.py:294
  1183.5 15.4 copy-start.47
  1331.4 14.4 collective-permute-start.6
  1333.2 12.6 copy-start.12
  1333.2 12.6 collective-permute-start.7
  1362.7 286.7 %all-reduce.19.cloned.1.call-start = ((), (), s32[]{:S(2)}) async-start(), calls=%async_computation.8 | async-start | bytes 28311552 | tf_op jit(solution)/shard_map/psum | solution.py:294
  1365.4 358.9 %all-reduce.13.cloned.1.call-start = ((), (), s32[]{:S(2)}) async-start(), calls=%async_computation.5 | async-start | bytes 237568 | tf_op jit(solution)/shard_map/psum | solution.py:293
  1396.6 776.1 %all-reduce.15.cloned.1.call-start = ((), (), s32[]{:S(2)}) async-start(), calls=%async_computation.6 | async-start | bytes 28311552 | tf_op jit(solution)/shard_map/psum | solution.py:293
  1650.1 28.7 %slice-start.2 = ((s8[6291456]{0:T(1024)(128)(4,1)}), s8[4194304]{0:T(1024)(128)(4,1)S(1)}, s32[]{:S(2)}) async-start(s8[6291456]{0:T(1024)(128)(4,1)} %bitcast.184), calls=%async_computation.11 | async-start | bytes 8388608
  1650.1 28.7 %slice-start.4 = ((s8[6291456]{0:T(1024)(128)(4,1)}), s8[4194304]{0:T(1024)(128)(4,1)S(1)}, s32[]{:S(2)}) async-start(s8[6291456]{0:T(1024)(128)(4,1)} %bitcast.193), calls=%async_computation.13 | async-start | bytes 8388608
  1650.1 28.7 %slice-start.3 = ((s8[6291456]{0:T(1024)(128)(4,1)}), s8[2097152]{0:T(1024)(128)(4,1)S(1)}, s32[]{:S(2)}) async-start(s8[6291456]{0:T(1024)(128)(4,1)} %bitcast.184), calls=%async_computation.12 | async-start | bytes 4194304
  1650.1 28.7 %slice-start.5 = ((s8[6291456]{0:T(1024)(128)(4,1)}), s8[2097152]{0:T(1024)(128)(4,1)S(1)}, s32[]{:S(2)}) async-start(s8[6291456]{0:T(1024)(128)(4,1)} %bitcast.193), calls=%async_computation.14 | async-start | bytes 4194304
  1654.7 24.1 %copy-start.3 = (bf16[16,8,32,384]{3,2,1,0:T(8,128)(2,1)S(1)}, bf16[16,8,32,384]{3,2,1,0:T(8,128)(2,1)}, u32[]{:S(2)}) copy-start(bf16[16,8,32,384]{3,2,1,0:T(8,128)(2,1)} %param.15) | copy-start | bytes 9437188
  2172.7 11.8 copy-start.58
  2172.7 12.4 copy-start.19
  (81 other events, 444.5 us)
Sparse Core Ops, SparseCore 0:
  52.0 167.2 all-gather.1
  1104.2 197.1 reduce-scatter.4
  1362.8 33.6 all-reduce.16
  1400.7 248.6 all-reduce.18
  1653.3 70.8 all-reduce.12
  1730.3 442.2 all-reduce.14
